TPU v7x, 32 devices: a whole 2x2x4 slice. The times are simulated.
32 devices in a mesh: order: 2 (over core), tok: 16 (over z, y, x).
Axes of the slice: x: 2, y: 2, z: 4, core: 2. Of those that a mesh axis runs over, the one named last changes fastest.
Arguments:
- queries: bfloat16 [65536, 512], P(('order', 'tok')), may hold values from -6 to 6
- key_tokens: bfloat16 [65536, 512], P(('order', 'tok')), may hold values from -6 to 6
- value_tokens: bfloat16 [65536, 512], P(('order', 'tok')), may hold values from -6 to 6
- learn_rates: float32 [65536], P(('order', 'tok')), may hold values from 0.02 to 0.2
- fast_init: float32 [512, 1536], replicated, may hold values from -0.25 to 0.25
- out_gain: float32 [512], replicated, may hold values from 0.5 to 1.5
Outputs:
- output: bfloat16 [65536, 512], P(('order', 'tok'))
All inputs are finite; a program needn't handle non-finite values.
Results may differ from a plain program's by a relative error of at most 0.015.
Values may be sent and summed in bfloat16 or wider, within the bound.
A program may use at most 128 MiB of HBM per device.

v0:
```python
import jax
import jax.numpy as jnp
from jax import lax
from jax.sharding import PartitionSpec as P


def prefix(x, axis, join, neutral):
    place = lax.axis_index(axis)
    gathered = lax.all_gather(x.astype(jnp.bfloat16), axis)
    state = jnp.zeros_like(x) + jnp.asarray(neutral, x.dtype)

    def one(lap, state):
        return join(state, lax.dynamic_index_in_dim(gathered, lap, 0, False).astype(x.dtype))

    return lax.fori_loop(0, place, one, state)


def gate_up(rows_in, weights_bf):
    width = weights_bf.shape[0]
    both_parts = jnp.dot(rows_in, weights_bf[:, : 2 * width], preferred_element_type=jnp.float32)
    return (both_parts[:, :width], both_parts[:, width:])


def backward_terms(key_rows, target, weights_bf):
    width = weights_bf.shape[0]
    gate_pre, up_pre = gate_up(key_rows, weights_bf)
    squash = jax.nn.sigmoid(gate_pre)
    activated = gate_pre * squash
    hidden = (activated * up_pre).astype(jnp.bfloat16)
    hidden_grad = lax.dot_general(
        target,
        weights_bf[:, 2 * width :],
        (((1,), (1,)), ((), ())),
        preferred_element_type=jnp.float32,
    )
    gate_grad = (hidden_grad * up_pre * squash * (1.0 + gate_pre * (1.0 - squash))).astype(
        jnp.bfloat16
    )
    up_grad = (hidden_grad * activated).astype(jnp.bfloat16)
    return (hidden, jnp.concatenate([gate_grad, up_grad], axis=1))


def local_term(key_rows, hidden, inner_grads, target):
    upper = lax.dot_general(
        key_rows, inner_grads, (((0,), (0,)), ((), ())), preferred_element_type=jnp.float32
    )
    lower = lax.dot_general(
        hidden, target, (((0,), (0,)), ((), ())), preferred_element_type=jnp.float32
    )
    return jnp.concatenate([upper, lower], axis=1)


def summed_whole(key_rows, target, weights_bf):
    hidden, inner_grads = backward_terms(key_rows, target, weights_bf)
    return lax.psum(local_term(key_rows, hidden, inner_grads, target), "tok")


def accumulate(earlier, later):
    return earlier + later


def apply_weights(query_rows, weights_bf, out_gain):
    width = weights_bf.shape[0]
    gate_pre, up_pre = gate_up(query_rows, weights_bf)
    hidden = (jax.nn.silu(gate_pre) * up_pre).astype(jnp.bfloat16)
    result = jnp.dot(hidden, weights_bf[:, 2 * width :], preferred_element_type=jnp.float32)
    norm_inv = lax.rsqrt(jnp.mean(result * result, axis=1, keepdims=True) + 1e-06)
    return (result * norm_inv * out_gain[None, :]).astype(jnp.bfloat16)


def shards(queries, key_tokens, value_tokens, learn_rates, fast_init, out_gain):
    group_rows = key_tokens.shape[0] * lax.axis_size("tok")
    factor = group_rows ** (-0.5)
    target = (-(learn_rates[:, None] * factor) * value_tokens.astype(jnp.float32)).astype(
        jnp.bfloat16
    )
    first_step = fast_init - summed_whole(key_tokens, target, fast_init.astype(jnp.bfloat16))
    second_step = first_step - summed_whole(key_tokens, target, first_step.astype(jnp.bfloat16))
    change = second_step - fast_init
    earlier = prefix(change, "order", accumulate, jnp.zeros_like(change))
    closing_bf = (fast_init + earlier + change).astype(jnp.bfloat16)
    return apply_weights(queries, closing_bf, out_gain)


def solution(mesh):
    return jax.shard_map(
        shards,
        mesh=mesh,
        in_specs=(
            P(("order", "tok"), None),
            P(("order", "tok"), None),
            P(("order", "tok"), None),
            P(("order", "tok")),
            P(),
            P(),
        ),
        out_specs=P(("order", "tok"), None),
        check_vma=False,
    )
```

profile of v0, /device:TPU:1, one launch (start us, length us, event | category | flops | bytes accessed | tf_op | source)
XLA Modules:
  0.0 383.2 jit_solution(1011616236271366115)
XLA Ops:
  6.5 0.8 multiply_negate_fusion
  7.4 2.1 convert_element_type.50
  9.5 2.4 fusion.24
  11.9 2.9 multiply_convert_fusion.6
  14.8 2.1 fusion.11
  16.9 2.3 fusion.18
  19.2 2.0 pad_maximum_fusion
  21.2 0.0 all-reduce.3.cloned.1.call-update
  21.2 0.2 all-reduce.5.cloned.1.call-start
  21.5 3.5 copy.10
  25.0 145.2 %all-reduce.3.cloned.1.call-done = f32[512,1536]{0,1:T(8,128)} async-done(((f32[512,1536]{0,1:T(8,128)}), f32[512,1536]{0,1:T(8,128)}) %all-reduce.3.cloned.1.call-update) | async-done | bytes 3145744 | tf_op jit(solution)/shard_map/psum | solution.py:55
  170.2 5.3 %fusion.38 = (bf16[512,1536]{0,1:T(8,128)(2,1)S(1)}, f32[512,1536]{0,1:T(8,128)}) fusion(f32[512,1536]{0,1:T(8,128)} %copy.10, f32[512,1536]{0,1:T(8,128)} %all-reduce.3.cloned.1.call-done), kind=kLoop, calls=%fused_computation.52 | loop fusion | flops 1572864 | bytes 11010048 | tf_op jit(solution)/shard_map/convert_element_type | solution.py:78
  175.5 2.4 convolution_bitcast_fusion.1
  177.9 3.2 multiply_convert_fusion.3
  181.1 2.1 fusion.12
  183.2 2.3 fusion.15
  185.6 2.0 pad_maximum_fusion.1
  187.5 0.0 all-reduce.5.cloned.1.call-update
  187.5 0.0 all-gather.3.cloned.1.call-start
  187.6 146.1 %all-reduce.5.cloned.1.call-done = f32[512,1536]{0,1:T(8,128)} async-done(((f32[512,1536]{0,1:T(8,128)}), f32[512,1536]{0,1:T(8,128)}) %all-reduce.5.cloned.1.call-update) | async-done | bytes 3145744 | tf_op jit(solution)/shard_map/psum | solution.py:55
  333.7 4.9 %fusion.21 = bf16[512,1536]{0,1:T(8,128)(2,1)} fusion(f32[512,1536]{0,1:T(8,128)S(1)} %copy-done.2, f32[512,1536]{0,1:T(8,128)} %get-tuple-element.42, f32[512,1536]{0,1:T(8,128)} %all-reduce.5.cloned.1.call-done), kind=kLoop, calls=%fused_computation.35 | loop fusion | flops 2359296 | bytes 11010048 | tf_op jit(solution)/shard_map/convert_element_type | solution.py:9
  338.6 12.0 %all-gather.3.cloned.1.call-done = bf16[1024,1536]{0,1:T(8,128)(2,1)} async-done(((bf16[512,1536]{0,1:T(8,128)(2,1)}), bf16[1024,1536]{0,1:T(8,128)(2,1)}) %all-gather.3.cloned.1.call-update) | async-done | bytes 3145744 | tf_op jit(solution)/shard_map/all_gather | solution.py:9
  350.6 4.6 %copy.13 = bf16[1024,1536]{1,0:T(8,128)(2,1)} copy(bf16[1024,1536]{0,1:T(8,128)(2,1)} %all-gather.3.cloned.1.call-done) | data formatting | bytes 6291456 | tf_op jit(solution)/shard_map/while | solution.py:15
  355.2 0.4 broadcast_in_dim.2
  355.6 2.5 while.10
  355.7 2.2 convert_add_fusion.2
  358.1 2.4 copy.11
  360.5 6.4 %add_convert_fusion = bf16[512,1536]{0,1:T(8,128)(2,1)S(1)} fusion(f32[512,1536]{0,1:T(8,128)} %copy.10, f32[512,1536]{0,1:T(8,128)} %copy.11, f32[512,1536]{0,1:T(8,128)} %get-tuple-element.42, f32[512,1536]{0,1:T(8,128)} %all-reduce.5.cloned.1.call-done), kind=kLoop, calls=%fused_computation.28 | loop fusion | flops 3932160 | bytes 14155776 | tf_op jit(solution)/shard_map/convert_element_type | solution.py:81
  366.8 2.4 convolution_bitcast_fusion
  369.2 1.7 multiply_reduce_fusion
  371.0 1.7 multiply_convert_fusion
  372.7 3.9 %copy.12 = bf16[2048,512]{1,0:T(8,128)(2,1)} copy(bf16[2048,512]{0,1:T(8,128)(2,1)} %multiply_convert_fusion) | data formatting | bytes 4194304 | tf_op jit(solution)/shard_map/convert_element_type | solution.py:68
  (17 shorter events, 0.1 us)
Async XLA Ops:
  6.5 2.9 copy-start
  6.5 163.7 %all-reduce.3.cloned.1.call-start = ((), (), s32[]{:S(2)}) async-start(), calls=%async_computation | async-start | bytes 6291456 | tf_op jit(solution)/shard_map/psum | solution.py:55
  9.5 2.5 copy-start.4
  21.2 312.4 %all-reduce.5.cloned.1.call-start = ((), (), s32[]{:S(2)}) async-start(), calls=%async_computation.1 | async-start | bytes 6291456 | tf_op jit(solution)/shard_map/psum | solution.py:55
  175.5 2.4 copy-start.5
  187.5 146.2 %copy-start.2 = (f32[512,1536]{0,1:T(8,128)S(1)}, f32[512,1536]{0,1:T(8,128)}, u32[]{:S(2)}) copy-start(f32[512,1536]{0,1:T(8,128)} %copy.10) | copy-start | bytes 9437188
  187.5 163.1 %all-gather.3.cloned.1.call-start = ((), (), s32[]{:S(2)}) async-start(), calls=%async_computation.2 | async-start | bytes 4718592 | tf_op jit(solution)/shard_map/all_gather | solution.py:9
  360.5 6.4 %copy-start.6 = (bf16[2048,512]{1,0:T(8,128)(2,1)S(1)}, bf16[2048,512]{1,0:T(8,128)(2,1)}, u32[]{:S(2)}) copy-start(bf16[2048,512]{1,0:T(8,128)(2,1)} %param.8) | copy-start | bytes 6291460
  369.2 1.7 copy-start.3
  371.0 5.7 %copy-start.1 = (bf16[2048,512]{1,0:T(8,128)(2,1)S(1)}, bf16[2048,512]{1,0:T(8,128)(2,1)}, u32[]{:S(2)}) copy-start(bf16[2048,512]{1,0:T(8,128)(2,1)} %param.9) | copy-start | bytes 6291460
Sparse Core Ops, SparseCore 0:
  21.4 148.7 all-reduce.2
  187.7 145.9 all-reduce.4
  338.7 11.8 all-gather.2
where the time goes:
time: 383 us
  waiting for transfers between devices  303 us (79%)
  other arithmetic  27.4 us (7%)
  matrix products  23.9 us (6%)
  local copies, waits for them, and re-layouts  14.8 us (4%)
  between operations  13.3 us (3%)
    psum x2, waiting for transfers between devices, summed_whole(): return lax.psum(local_term(key_rows, hidden, inner_grads, target), 'tok')  291 us
    all_gather x1, waiting for transfers between devices, prefix(): gathered = lax.all_gather(x.astype(jnp.bfloat16), axis)  12 us
  transfers between devices with their start and end apart: 3, of which 3 were waited for; matrix products, arithmetic and copies ran while one was open for 1% of the time, Pallas kernels for 0%

commit v1 on v0

--- a/solution.py
+++ b/solution.py
@@ -2,6 +2,12 @@
 import jax.numpy as jnp
 from jax import lax
 from jax.sharding import PartitionSpec as P
+
+
+def summed_here(x, name):
+    pieces = lax.all_gather(x, name, axis=0, tiled=False)
+    summed = pieces.sum(axis=0)
+    return summed
 
 
 def prefix(x, axis, join, neutral):
@@ -52,7 +58,7 @@
 
 def summed_whole(key_rows, target, weights_bf):
     hidden, inner_grads = backward_terms(key_rows, target, weights_bf)
-    return lax.psum(local_term(key_rows, hidden, inner_grads, target), "tok")
+    return summed_here(local_term(key_rows, hidden, inner_grads, target), "tok")
 
 
 def accumulate(earlier, later):

time: 383 us -> 1290 us (3.37)
  waiting for transfers between devices: 303 us -> 1060 us
  local copies, waits for them, and re-layouts: 14.8 us -> 121 us
  other arithmetic: 27.4 us -> 65.4 us
    all_gather x0 -> x2, waiting for transfers between devices: none -> 1050 us  [summed_here(): pieces = lax.all_gather(x, name, axis=0, tiled=False)]
    psum x2 -> x0, waiting for transfers between devices: 291 us -> none  [summed_whole(): return lax.psum(local_term(key_rows, hidden, inner_grads, target), 'tok')]
    unnamed x15 -> x19, local copies, waits for them, and re-layouts: 3.55 us -> 107 us
    reduce_sum x0 -> x2, other arithmetic: none -> 36.8 us  [summed_here(): summed = pieces.sum(axis=0)]
  transfers between devices with their start and end apart: 3 -> 3, of which waited for: 3 -> 3; matrix products, arithmetic and copies ran while one was open for 1% -> 0% of each run, Pallas kernels for 0% -> 0%
where the time goes in v1:
time: 1290 us
  waiting for transfers between devices  1060 us (82%)
  local copies, waits for them, and re-layouts  121 us (9%)
  other arithmetic  65.4 us (5%)
  matrix products  24.1 us (2%)
  between operations  13.3 us (1%)
    all_gather x2, waiting for transfers between devices, summed_here(): pieces = lax.all_gather(x, name, axis=0, tiled=False)  1050 us
    unnamed x19, local copies, waits for them, and re-layouts  107 us
    reduce_sum x2, other arithmetic, summed_here(): summed = pieces.sum(axis=0)  36.8 us
  transfers between devices with their start and end apart: 3, of which 3 were waited for; matrix products, arithmetic and copies ran while one was open for 0% of the time, Pallas kernels for 0%

profile of v1, /device:TPU:1, one launch (start us, length us, event | category | flops | bytes accessed | tf_op | source)
XLA Modules:
  0.0 1289.2 jit_solution(4921157280094394612)
XLA Ops:
  6.5 0.8 multiply_negate_fusion
  7.4 2.1 convert_element_type.50
  9.5 2.4 fusion.24
  11.9 2.9 multiply_convert_fusion.6
  14.8 2.1 fusion.11
  16.9 2.3 fusion.18
  19.2 1.9 pad_maximum_fusion
  21.4 3.5 copy.11
  25.0 526.0 %all-gather.7.cloned.1.call-done = f32[8192,1536]{0,1:T(8,128)} async-done(((f32[512,1536]{0,1:T(8,128)}), f32[8192,1536]{0,1:T(8,128)}) %all-gather.7.cloned.1.call-update) | async-done | bytes 50331664 | tf_op jit(solution)/shard_map/all_gather | solution.py:8
  551.0 51.8 %copy.15 = f32[192,8,16,512]{3,2,1,0:T(8,128)} copy(f32[192,8,16,512]{3,1,2,0:T(8,128)} %bitcast.29) | data formatting | bytes 100663296
  602.8 18.4 %bitcast_reduce_fusion.1 = f32[512,1536]{0,1:T(8,128)} fusion(f32[192,8,16,512]{3,2,1,0:T(8,128)} %copy.15), kind=kLoop, calls=%fused_computation.2 | loop fusion | flops 11796480 | bytes 53477376 | tf_op jit(solution)/shard_map/reduce_sum | solution.py:9
  621.2 4.3 fusion.38
  625.5 2.4 convolution_bitcast_fusion.1
  627.8 3.4 multiply_convert_fusion.3
  631.3 2.1 fusion.12
  633.4 2.3 fusion.15
  635.7 1.9 pad_maximum_fusion.1
  637.8 526.9 %all-gather.9.cloned.1.call-done = f32[8192,1536]{0,1:T(8,128)} async-done(((f32[512,1536]{0,1:T(8,128)}), f32[8192,1536]{0,1:T(8,128)}) %all-gather.9.cloned.1.call-update) | async-done | bytes 50331664 | tf_op jit(solution)/shard_map/all_gather | solution.py:8
  1164.7 51.8 %copy.16 = f32[192,8,16,512]{3,2,1,0:T(8,128)} copy(f32[192,8,16,512]{3,1,2,0:T(8,128)} %bitcast.30) | data formatting | bytes 100663296
  1216.5 18.4 %bitcast_reduce_fusion = f32[512,1536]{0,1:T(8,128)} fusion(f32[192,8,16,512]{3,2,1,0:T(8,128)} %copy.16), kind=kLoop, calls=%fused_computation.1 | loop fusion | flops 11796480 | bytes 53477376 | tf_op jit(solution)/shard_map/reduce_sum | solution.py:9
  1234.9 4.9 fusion.21
  1239.8 11.9 all-gather.11.cloned.1.call-done
  1251.7 4.7 copy.14
  1256.4 2.1 broadcast_in_dim.2
  1258.5 4.5 while.10
  1258.5 4.5 convert_add_fusion.2
  1263.0 3.5 copy.12
  1266.6 6.4 add_convert_fusion
  1272.9 2.4 convolution_bitcast_fusion
  1275.3 1.7 multiply_reduce_fusion
  1277.1 1.7 multiply_convert_fusion
  1278.8 3.9 copy.13
  (23 shorter events, 0.4 us)
Async XLA Ops:
  6.5 2.9 copy-start
  6.5 544.4 %all-gather.7.cloned.1.call-start = ((), (), s32[]{:S(2)}) async-start(), calls=%async_computation | async-start | bytes 53477376 | tf_op jit(solution)/shard_map/all_gather | solution.py:8
  9.5 2.5 copy-start.5
  21.2 1143.5 %all-gather.9.cloned.1.call-start = ((), (), s32[]{:S(2)}) async-start(), calls=%async_computation.1 | async-start | bytes 53477376 | tf_op jit(solution)/shard_map/all_gather | solution.py:8
  602.8 18.4 %copy-start.2 = (f32[512,1536]{0,1:T(8,128)S(1)}, f32[512,1536]{0,1:T(8,128)}, u32[]{:S(2)}) copy-start(f32[512,1536]{0,1:T(8,128)} %copy.11) | copy-start | bytes 9437188
  625.4 2.4 copy-start.6
  637.7 614.0 %all-gather.11.cloned.1.call-start = ((), (), s32[]{:S(2)}) async-start(), calls=%async_computation.2 | async-start | bytes 4718592 | tf_op jit(solution)/shard_map/all_gather | solution.py:15
  1216.5 18.4 %copy-start.3 = (f32[512,1536]{0,1:T(8,128)S(1)}, f32[512,1536]{0,1:T(8,128)}, u32[]{:S(2)}) copy-start(f32[512,1536]{0,1:T(8,128)} %copy.11) | copy-start | bytes 9437188
  1266.6 6.4 copy-start.7
  1275.3 1.7 copy-start.4
  1277.0 5.7 copy-start.1
Sparse Core Ops, SparseCore 0:
  21.3 529.5 all-gather.6
  637.8 526.8 all-gather.8
  1239.9 11.7 all-gather.10
